TPU v7x, 512 devices: a whole 4x4x16 slice. The times are simulated.
512 devices in a mesh: dp: 32 (over x, z_lo, core), tensor: 16 (over z_hi, y).
Axes of the slice: x: 4, y: 4, z: 16 (z_hi: 4, z_lo: 4; z = z_hi * 4 + z_lo), core: 2. Of those that a mesh axis runs over, the one named last changes fastest.
Arguments:
- page_patches: bfloat16 [32768, 6144], P('dp', 'tensor'), may hold values from -720 to 720
- gain: bfloat16 [6144], P('tensor'), may hold values from 0.5 to 1.5
- q_weight: bfloat16 [6144, 4096], P('dp', 'tensor'), may hold values from -0.076546554 to 0.076546554
- k_weight: bfloat16 [6144, 4096], P('dp', 'tensor'), may hold values from -2.0412415 to 2.0412415
- v_weight: bfloat16 [6144, 4096], P('dp', 'tensor'), may hold values from -0.078125 to 0.078125
- pack_lengths: int32 [32, 32], replicated, may hold values from 1 to 32, 512 in all within a row
- line_order: int32 [32, 32], replicated, may hold values from 0 to 31, each once within a row
Outputs:
- context: bfloat16 [16384, 4096], P('dp', 'tensor')
Inputs may be any that keep to these rules, and one draw needn't show every extreme that they name: `pack_lengths`: every row sums to exactly 512 and holds the value 32. `line_order`: each row names every sequence 0 to 31 once.
All inputs are finite; a program needn't handle non-finite values.
Results may differ from a plain program's by a relative error of at most 0.0079.
Values may be sent and summed in bfloat16 or wider, within the bound.
No kernel may reach another device: no remote copies, remote signals or barrier semaphores. Data moves between devices by JAX's collectives and lax.ppermute only.
A program may use at most 64 MiB of HBM per device.

v0:
```python
import math
import jax
import jax.numpy as jnp
from jax import lax
from jax.sharding import PartitionSpec as P

HEAD_DIM = 128
norm_epsilon = 1e-06


def shards(page_patches, gain, q_weight, k_weight, v_weight, pack_lengths, line_order):
    groups = lax.axis_size("dp")
    page_index = lax.axis_index("dp")
    feature_cols = page_patches.shape[1]
    slot_rows = page_patches.shape[0] // groups
    seq_rows = slot_rows * groups // 2
    targets = jnp.arange(groups, dtype=jnp.int32)
    my_order = lax.dynamic_index_in_dim(line_order, page_index, 0, keepdims=False)
    slot_for = jnp.sum(
        jnp.where(my_order[None, :] == targets[:, None], targets[None, :], 0), axis=1
    )
    slots = page_patches.reshape(groups, slot_rows, feature_cols)
    outgoing = jnp.take(slots, slot_for, axis=0)
    incoming = lax.all_to_all(outgoing, "dp", split_axis=0, concat_axis=0, tiled=True)
    my_lengths = lax.dynamic_index_in_dim(pack_lengths, page_index, 0, keepdims=False)
    line_ends = jnp.cumsum(my_lengths)
    line_starts = line_ends - my_lengths
    places = jnp.arange(seq_rows, dtype=jnp.int32)
    segment = jnp.sum((line_ends[None, :] <= places[:, None]).astype(jnp.int32), axis=1)
    start_of_row = jnp.sum(
        jnp.where(segment[:, None] == targets[None, :], line_starts[None, :], 0), axis=1
    )
    source_rows = segment * slot_rows + places - start_of_row
    packed = jnp.take(incoming.reshape(groups * slot_rows, feature_cols), source_rows, axis=0)
    full_rows, full_gain = (
        lax.all_gather(packed, "tensor", axis=1, tiled=True),
        lax.all_gather(gain, "tensor", axis=0, tiled=True),
    )
    row_vals = full_rows.astype(jnp.float32)
    row_mean = jnp.mean(row_vals, axis=1, keepdims=True)
    row_var = jnp.mean(jnp.square(row_vals - row_mean), axis=1, keepdims=True)
    normed = (
        (row_vals - row_mean) * lax.rsqrt(row_var + norm_epsilon) * full_gain.astype(jnp.float32)
    ).astype(jnp.bfloat16)
    pieces = (
        lax.all_gather(q_weight, "dp", axis=0, tiled=True),
        lax.all_gather(k_weight, "dp", axis=0, tiled=True),
        lax.all_gather(v_weight, "dp", axis=0, tiled=True),
    )
    query_sum, key_sum, value_sum = tuple(
        (jnp.dot(normed, weight_rows, preferred_element_type=jnp.float32) for weight_rows in pieces)
    )
    local_heads = q_weight.shape[1] // HEAD_DIM
    query_heads = query_sum.astype(jnp.bfloat16).reshape(seq_rows, local_heads, HEAD_DIM)
    key_heads = key_sum.astype(jnp.bfloat16).reshape(seq_rows, local_heads, HEAD_DIM)
    value_heads = value_sum.astype(jnp.bfloat16).reshape(seq_rows, local_heads, HEAD_DIM)
    scores = jnp.einsum(
        "qhd,khd->hqk", query_heads, key_heads, preferred_element_type=jnp.float32
    ) * (1.0 / math.sqrt(HEAD_DIM))
    same_line = segment[:, None] == segment[None, :]
    scores = jnp.where(same_line[None, :, :], scores, -jnp.inf)
    row_max = jnp.max(scores, axis=2, keepdims=True)
    expo = jnp.exp(scores - row_max)
    attn_probs = (expo / jnp.sum(expo, axis=2, keepdims=True)).astype(jnp.bfloat16)
    context = jnp.einsum(
        "hqk,khd->qhd", attn_probs, value_heads, preferred_element_type=jnp.float32
    )
    return context.astype(jnp.bfloat16).reshape(seq_rows, local_heads * HEAD_DIM)


def solution(mesh):
    return jax.shard_map(
        shards,
        mesh=mesh,
        in_specs=(
            P("dp", "tensor"),
            P("tensor"),
            P("dp", "tensor"),
            P("dp", "tensor"),
            P("dp", "tensor"),
            P(),
            P(),
        ),
        out_specs=P("dp", "tensor"),
        check_vma=False,
    )
```

profile of v0, /device:TPU:1, one launch (start us, length us, event | category | flops | bytes accessed | tf_op | source)
XLA Modules:
  0.0 443.6 jit_solution(14901982915176972839)
XLA Ops:
  6.5 0.0 copy-start
  6.5 0.8 dynamic-slice_bitcast_fusion
  7.3 0.1 select_reduce_fusion.1
  7.5 0.2 copy-done
  7.7 0.7 gather_fusion
  8.4 1.0 broadcast_select_fusion
  9.4 0.0 copy-start.2
  9.4 10.6 %all-to-all-start = ((bf16[32,32,384]{2,1,0:T(8,128)(2,1)}), bf16[32,32,384]{2,1,0:T(8,128)(2,1)S(1)}, u32[]{:S(2)}, u32[]{:S(2)}) async-start(bf16[32,32,384]{2,1,0:T(8,128)(2,1)} %broadcast_select_fusion), calls=%async_computation | async-start | bytes 1572864 | tf_op jit(solution)/shard_map/all_to_all | solution.py:24
  20.0 0.0 all-gather.6.cloned.1.call-start
  20.1 0.7 fusion.17
  20.8 0.1 copy.23
  20.9 0.1 reduce-window.4
  20.9 0.1 reduce
  21.0 0.1 convert_reduce_fusion.1
  21.1 0.7 fusion.13
  21.8 0.1 select_reduce_fusion
  22.0 20.5 %all-to-all-done = bf16[32,32,384]{2,1,0:T(8,128)(2,1)S(1)} async-done(((bf16[32,32,384]{2,1,0:T(8,128)(2,1)}), bf16[32,32,384]{2,1,0:T(8,128)(2,1)S(1)}, u32[]{:S(2)}, u32[]{:S(2)}) %all-to-all-start) | async-done | bytes 786464 | tf_op jit(solution)/shard_map/all_to_all | solution.py:24
  42.5 1.9 gather_fusion.1
  44.4 0.9 broadcast_select_fusion.1
  45.3 0.0 all-gather.6.cloned.1.call-update
  45.3 0.0 all-gather.10.cloned.1.call-start
  45.4 0.7 all-gather.10.cloned.1.call-update
  46.1 0.0 all-gather.12.cloned.1.call-start
  46.1 0.7 all-gather.12.cloned.1.call-update
  46.8 0.0 all-gather.8.cloned.1.call-start
  46.9 0.5 all-gather.8.cloned.1.call-update
  47.4 0.0 copy-done.2
  47.4 49.9 %all-gather = bf16[16,1,384]{2,1,0:T(2,128)(2,1)S(1)} all-gather(bf16[1,1,384]{2,1,0:T(2,128)(2,1)S(1)} %reshape.150), channel_id=1, replica_groups=mesh['dp'=32,'tensor'=16] {'tensor'}, dimensions={0}, use_global_device_ids=true | all-gather | bytes 13056 | tf_op jit(solution)/shard_map/all_gather | solution.py:37
  97.4 0.2 broadcast_compare_fusion
  97.6 133.5 %all-gather.6.cloned.1.call-done = bf16[512,6144]{1,0:T(8,128)(2,1)} async-done(((bf16[512,384]{1,0:T(8,128)(2,1)}), bf16[512,6144]{1,0:T(8,128)(2,1)}) %all-gather.6.cloned.1.call-update) | async-done | bytes 6291472 | tf_op jit(solution)/shard_map/all_gather | solution.py:36
  231.1 0.0 copy-start.1
  231.1 3.8 convert_reduce_fusion
  234.9 0.7 copy-done.1
  235.7 1.8 fusion.3
  237.5 6.3 %fusion.5 = bf16[512,6144]{1,0:T(8,128)(2,1)} fusion(bf16[512,6144]{1,0:T(8,128)(2,1)S(1)} %copy-done.1, f32[6144]{0:T(1024)S(1)} %bitcast.40, f32[512]{0:T(512)S(1)} %add_rsqrt_fusion, f32[512]{0:T(512)S(1)} %broadcast_multiply_fusion), kind=kLoop, calls=%fused_computation.9 | loop fusion | flops 15728640 | bytes 12611584 | tf_op jit(solution)/shard_map/convert_element_type | solution.py:44
  243.7 50.1 %all-gather.10.cloned.1.call-done = bf16[6144,256]{1,0:T(8,128)(2,1)} async-done(((bf16[192,256]{1,0:T(8,128)(2,1)}), bf16[6144,256]{1,0:T(8,128)(2,1)}) %all-gather.10.cloned.1.call-update) | async-done | bytes 3145744 | tf_op jit(solution)/shard_map/all_gather | solution.py:46
  293.8 5.5 %convolution_convert_fusion.1 = bf16[512,256]{0,1:T(8,128)(2,1)S(1)} fusion(bf16[512,6144]{1,0:T(8,128)(2,1)} %fusion.5, bf16[6144,256]{1,0:T(8,128)(2,1)} %all-gather.10.cloned.1.call-done), kind=kOutput, calls=%fused_computation.15 | convolution fusion | flops 1610743808 | bytes 9699328 | tf_op jit(solution)/shard_map/dot_general | solution.py:51
  299.4 62.3 %all-gather.12.cloned.1.call-done = bf16[6144,256]{1,0:T(8,128)(2,1)} async-done(((bf16[192,256]{1,0:T(8,128)(2,1)}), bf16[6144,256]{1,0:T(8,128)(2,1)}) %all-gather.12.cloned.1.call-update) | async-done | bytes 3145744 | tf_op jit(solution)/shard_map/all_gather | solution.py:47
  361.7 5.5 %convolution_convert_fusion = bf16[512,256]{0,1:T(8,128)(2,1)S(1)} fusion(bf16[512,6144]{1,0:T(8,128)(2,1)} %fusion.5, bf16[6144,256]{1,0:T(8,128)(2,1)} %all-gather.12.cloned.1.call-done), kind=kOutput, calls=%fused_computation.14 | convolution fusion | flops 1610743808 | bytes 9699328 | tf_op jit(solution)/shard_map/dot_general | solution.py:51
  367.2 1.0 fusion.21
  368.2 61.2 %all-gather.8.cloned.1.call-done = bf16[6144,256]{1,0:T(8,128)(2,1)} async-done(((bf16[192,256]{1,0:T(8,128)(2,1)}), bf16[6144,256]{1,0:T(8,128)(2,1)}) %all-gather.8.cloned.1.call-update) | async-done | bytes 3145744 | tf_op jit(solution)/shard_map/all_gather | solution.py:48
  429.4 5.5 %convolution_convert_fusion.2 = bf16[512,256]{0,1:T(8,128)(2,1)S(1)} fusion(bf16[512,6144]{1,0:T(8,128)(2,1)} %fusion.5, bf16[6144,256]{1,0:T(8,128)(2,1)} %all-gather.8.cloned.1.call-done), kind=kOutput, calls=%fused_computation.16 | convolution fusion | flops 1610743808 | bytes 9699328 | tf_op jit(solution)/shard_map/dot_general | solution.py:51
  434.9 1.3 convolution_convert_fusion.3
  436.2 0.8 copy.27
  (11 shorter events, 0.1 us)
Async XLA Ops:
  6.5 1.1 copy-start
  9.4 38.0 %copy-start.2 = (bf16[384]{0:T(512)(128)(2,1)S(1)}, bf16[384]{0:T(512)(128)(2,1)}, u32[]{:S(2)}) copy-start(bf16[384]{0:T(512)(128)(2,1)} %param.8) | copy-start | bytes 2308
  9.4 33.0 %all-to-all-start = ((bf16[32,32,384]{2,1,0:T(8,128)(2,1)}), bf16[32,32,384]{2,1,0:T(8,128)(2,1)S(1)}, u32[]{:S(2)}, u32[]{:S(2)}) async-start(bf16[32,32,384]{2,1,0:T(8,128)(2,1)} %broadcast_select_fusion), calls=%async_computation | async-start | bytes 1572864 | tf_op jit(solution)/shard_map/all_to_all | solution.py:24
  20.0 211.1 %all-gather.6.cloned.1.call-start = ((), (), s32[]{:S(2)}) async-start(), calls=%async_computation.1 | async-start | bytes 6684672 | tf_op jit(solution)/shard_map/all_gather | solution.py:36
  45.3 248.5 %all-gather.10.cloned.1.call-start = ((), (), s32[]{:S(2)}) async-start(), calls=%async_computation.3 | async-start | bytes 3244032 | tf_op jit(solution)/shard_map/all_gather | solution.py:46
  46.1 315.6 %all-gather.12.cloned.1.call-start = ((), (), s32[]{:S(2)}) async-start(), calls=%async_computation.4 | async-start | bytes 3244032 | tf_op jit(solution)/shard_map/all_gather | solution.py:47
  46.8 382.6 %all-gather.8.cloned.1.call-start = ((), (), s32[]{:S(2)}) async-start(), calls=%async_computation.2 | async-start | bytes 3244032 | tf_op jit(solution)/shard_map/all_gather | solution.py:48
  231.1 4.6 %copy-start.1 = (bf16[512,6144]{1,0:T(8,128)(2,1)S(1)}, bf16[512,6144]{1,0:T(8,128)(2,1)}, u32[]{:S(2)}) copy-start(bf16[512,6144]{1,0:T(8,128)(2,1)} %all-gather.6.cloned.1.call-done) | copy-start | bytes 18874372
Sparse Core Ops, SparseCore 0:
  45.5 185.5 all-gather.5
  233.2 60.5 all-gather.9
  296.0 65.6 all-gather.11
  363.7 65.6 all-gather.7
where the time goes:
time: 444 us
  waiting for transfers between devices  329 us (74%)
  blocking collectives  49.9 us (11%)
  matrix products  18.8 us (4%)
  other arithmetic  15.3 us (3%)
  between operations  13.3 us (3%)
  starting transfers between devices  10.7 us (2%)
  local copies, waits for them, and re-layouts  6.03 us (1%)
    all_gather x1, waiting for transfers between devices, shards(): lax.all_gather(packed, 'tensor', axis=1, tiled=True)  133 us
    all_gather x1, waiting for transfers between devices, shards(): lax.all_gather(k_weight, 'dp', axis=0, tiled=True)  62.3 us
    all_gather x1, waiting for transfers between devices, shards(): lax.all_gather(v_weight, 'dp', axis=0, tiled=True)  61.2 us
    all_gather x1, waiting for transfers between devices, shards(): lax.all_gather(q_weight, 'dp', axis=0, tiled=True)  50.1 us
    all_gather x1, blocking collectives, shards(): lax.all_gather(gain, 'tensor', axis=0, tiled=True)  49.9 us
    all_to_all x1, waiting for transfers between devices, shards(): lax.all_to_all(outgoing, 'dp', split_axis=0, concat_axis=0, tiled=True)  20.5 us
    dot_general x3, matrix products, shards(): jnp.dot(normed, weight_rows, preferred_element_type=jnp.float32)  16.6 us
    all_to_all x1, starting transfers between devices, shards(): lax.all_to_all(outgoing, 'dp', split_axis=0, concat_axis=0, tiled=True)  10.6 us
  transfers between devices with their start and end apart: 5, of which 5 were waited for; matrix products, arithmetic and copies ran while one was open for 6% of the time, Pallas kernels for 0%

commit v1 on v0

--- a/solution.py
+++ b/solution.py
@@ -6,6 +6,11 @@
 
 HEAD_DIM = 128
 norm_epsilon = 1e-06
+
+
+def all_by_exchange(x, mesh_axis, d):
+    outgoing = jnp.stack([x] * lax.axis_size(mesh_axis))
+    return jnp.concatenate(lax.all_to_all(outgoing, mesh_axis, 0, 0), axis=d)
 
 
 def shards(page_patches, gain, q_weight, k_weight, v_weight, pack_lengths, line_order):
@@ -44,7 +49,7 @@
     ).astype(jnp.bfloat16)
     pieces = (
         lax.all_gather(q_weight, "dp", axis=0, tiled=True),
-        lax.all_gather(k_weight, "dp", axis=0, tiled=True),
+        all_by_exchange(k_weight, "dp", 0),
         lax.all_gather(v_weight, "dp", axis=0, tiled=True),
     )
     query_sum, key_sum, value_sum = tuple(

time: 444 us -> 415 us (0.935)
  waiting for transfers between devices: 329 us -> 228 us
  blocking collectives: 49.9 us -> 116 us
  starting transfers between devices: 10.7 us -> 15.5 us
    all_gather x1, waiting for transfers between devices: 133 us -> 61.3 us  [shards(): lax.all_gather(packed, 'tensor', axis=1, tiled=True)]
    all_gather x1, blocking collectives: 49.9 us -> 116 us  [shards(): lax.all_gather(gain, 'tensor', axis=0, tiled=True)]
    all_gather x1 -> x0, waiting for transfers between devices: 62.3 us -> none  [shards(): lax.all_gather(k_weight, 'dp', axis=0, tiled=True)]
    all_gather x1, waiting for transfers between devices: 50.1 us -> 84 us  [shards(): lax.all_gather(q_weight, 'dp', axis=0, tiled=True)]
    all_to_all x0 -> x1, starting transfers between devices: none -> 4.77 us  [all_by_exchange(): return jnp.concatenate(lax.all_to_all(outgoing, mesh_axis, 0, 0), axis=d)]
  transfers between devices with their start and end apart: 5 -> 5, of which waited for: 5 -> 4; matrix products, arithmetic and copies ran while one was open for 6% -> 7% of each run, Pallas kernels for 0% -> 0%
where the time goes in v1:
time: 415 us
  waiting for transfers between devices  228 us (55%)
  blocking collectives  116 us (28%)
  matrix products  18.8 us (5%)
  starting transfers between devices  15.5 us (4%)
  other arithmetic  15.3 us (4%)
  between operations  13.3 us (3%)
  local copies, waits for them, and re-layouts  8.05 us (2%)
    all_gather x1, blocking collectives, shards(): lax.all_gather(gain, 'tensor', axis=0, tiled=True)  116 us
    all_gather x1, waiting for transfers between devices, shards(): lax.all_gather(q_weight, 'dp', axis=0, tiled=True)  84 us
    all_gather x1, waiting for transfers between devices, shards(): lax.all_gather(v_weight, 'dp', axis=0, tiled=True)  61.3 us
    all_gather x1, waiting for transfers between devices, shards(): lax.all_gather(packed, 'tensor', axis=1, tiled=True)  61.3 us
    all_to_all x1, waiting for transfers between devices, shards(): lax.all_to_all(outgoing, 'dp', split_axis=0, concat_axis=0, tiled=True)  20.5 us
    dot_general x3, matrix products, shards(): jnp.dot(normed, weight_rows, preferred_element_type=jnp.float32)  16.6 us
    all_to_all x1, starting transfers between devices, shards(): lax.all_to_all(outgoing, 'dp', split_axis=0, concat_axis=0, tiled=True)  10.6 us
  transfers between devices with their start and end apart: 5, of which 4 were waited for; matrix products, arithmetic and copies ran while one was open for 7% of the time, Pallas kernels for 0%

profile of v1, /device:TPU:1, one launch (start us, length us, event | category | flops | bytes accessed | tf_op | source)
XLA Modules:
  0.0 415.0 jit_solution(17850209419732960922)
XLA Ops:
  6.5 0.0 copy-start
  6.5 0.8 dynamic-slice_bitcast_fusion
  7.3 0.1 select_reduce_fusion.1
  7.5 0.2 copy-done
  7.7 0.7 gather_fusion
  8.4 1.0 broadcast_select_fusion
  9.4 0.0 copy-start.2
  9.4 10.6 %all-to-all-start = ((bf16[32,32,384]{2,1,0:T(8,128)(2,1)}), bf16[32,32,384]{2,1,0:T(8,128)(2,1)S(1)}, u32[]{:S(2)}, u32[]{:S(2)}) async-start(bf16[32,32,384]{2,1,0:T(8,128)(2,1)} %broadcast_select_fusion), calls=%async_computation | async-start | bytes 1572864 | tf_op jit(solution)/shard_map/all_to_all | solution.py:29
  20.0 0.0 all-gather.5.cloned.1.call-start
  20.1 0.7 fusion.17
  20.8 0.1 copy.23
  20.9 0.1 reduce-window.4
  20.9 0.1 reduce
  21.0 0.1 convert_reduce_fusion.1
  21.1 0.7 fusion.13
  21.8 0.1 select_reduce_fusion
  22.0 20.5 %all-to-all-done = bf16[32,32,384]{2,1,0:T(8,128)(2,1)S(1)} async-done(((bf16[32,32,384]{2,1,0:T(8,128)(2,1)}), bf16[32,32,384]{2,1,0:T(8,128)(2,1)S(1)}, u32[]{:S(2)}, u32[]{:S(2)}) %all-to-all-start) | async-done | bytes 786464 | tf_op jit(solution)/shard_map/all_to_all | solution.py:29
  42.5 1.9 gather_fusion.1
  44.4 0.9 broadcast_select_fusion.1
  45.3 0.0 all-gather.5.cloned.1.call-update
  45.3 0.0 copy-done.2
  45.3 2.0 stack.2
  47.4 0.0 copy-start.3
  47.4 4.8 %all-to-all-start.1 = ((bf16[32,192,256]{2,1,0:T(8,128)(2,1)}), bf16[32,192,256]{2,1,0:T(8,128)(2,1)}, u32[]{:S(2)}, u32[]{:S(2)}) async-start(bf16[32,192,256]{2,1,0:T(8,128)(2,1)} %stack.2), calls=%async_computation.1 | async-start | bytes 6291456 | tf_op jit(solution)/shard_map/all_to_all | solution.py:13
  52.1 0.0 all-gather.9.cloned.1.call-start
  52.2 0.7 all-gather.9.cloned.1.call-update
  52.9 0.0 all-gather.7.cloned.1.call-start
  52.9 0.7 all-gather.7.cloned.1.call-update
  53.6 0.0 copy-done.3
  53.7 115.6 %all-gather = bf16[16,1,384]{2,1,0:T(2,128)(2,1)S(1)} all-gather(bf16[1,1,384]{2,1,0:T(2,128)(2,1)S(1)} %reshape.156), channel_id=1, replica_groups=mesh['dp'=32,'tensor'=16] {'tensor'}, dimensions={0}, use_global_device_ids=true | all-gather | bytes 13056 | tf_op jit(solution)/shard_map/all_gather | solution.py:42
  169.3 0.2 broadcast_compare_fusion
  169.5 61.3 %all-gather.5.cloned.1.call-done = bf16[512,6144]{1,0:T(8,128)(2,1)} async-done(((bf16[512,384]{1,0:T(8,128)(2,1)}), bf16[512,6144]{1,0:T(8,128)(2,1)}) %all-gather.5.cloned.1.call-update) | async-done | bytes 6291472 | tf_op jit(solution)/shard_map/all_gather | solution.py:41
  230.8 0.0 copy-start.1
  230.8 3.8 convert_reduce_fusion
  234.7 0.7 copy-done.1
  235.4 1.8 fusion.3
  237.2 6.3 %fusion.5 = bf16[512,6144]{1,0:T(8,128)(2,1)} fusion(bf16[512,6144]{1,0:T(8,128)(2,1)S(1)} %copy-done.1, f32[6144]{0:T(1024)S(1)} %bitcast.41, f32[512]{0:T(512)S(1)} %add_rsqrt_fusion, f32[512]{0:T(512)S(1)} %broadcast_multiply_fusion), kind=kLoop, calls=%fused_computation.9 | loop fusion | flops 15728640 | bytes 12611584 | tf_op jit(solution)/shard_map/convert_element_type | solution.py:49
  243.5 0.0 all-to-all-done.1
  243.5 5.5 %convolution_convert_fusion = bf16[512,256]{0,1:T(8,128)(2,1)S(1)} fusion(bf16[512,6144]{1,0:T(8,128)(2,1)} %fusion.5, bf16[6144,256]{1,0:T(8,128)(2,1)} %bitcast.13), kind=kOutput, calls=%fused_computation.14 | convolution fusion | flops 1610743808 | bytes 9699328 | tf_op jit(solution)/shard_map/dot_general | solution.py:56
  249.0 84.0 %all-gather.9.cloned.1.call-done = bf16[6144,256]{1,0:T(8,128)(2,1)} async-done(((bf16[192,256]{1,0:T(8,128)(2,1)}), bf16[6144,256]{1,0:T(8,128)(2,1)}) %all-gather.9.cloned.1.call-update) | async-done | bytes 3145744 | tf_op jit(solution)/shard_map/all_gather | solution.py:51
  333.0 5.5 %convolution_convert_fusion.1 = bf16[512,256]{0,1:T(8,128)(2,1)S(1)} fusion(bf16[512,6144]{1,0:T(8,128)(2,1)} %fusion.5, bf16[6144,256]{1,0:T(8,128)(2,1)} %all-gather.9.cloned.1.call-done), kind=kOutput, calls=%fused_computation.15 | convolution fusion | flops 1610743808 | bytes 9699328 | tf_op jit(solution)/shard_map/dot_general | solution.py:56
  338.6 1.0 fusion.21
  339.5 61.3 %all-gather.7.cloned.1.call-done = bf16[6144,256]{1,0:T(8,128)(2,1)} async-done(((bf16[192,256]{1,0:T(8,128)(2,1)}), bf16[6144,256]{1,0:T(8,128)(2,1)}) %all-gather.7.cloned.1.call-update) | async-done | bytes 3145744 | tf_op jit(solution)/shard_map/all_gather | solution.py:53
  400.8 5.5 %convolution_convert_fusion.2 = bf16[512,256]{0,1:T(8,128)(2,1)S(1)} fusion(bf16[512,6144]{1,0:T(8,128)(2,1)} %fusion.5, bf16[6144,256]{1,0:T(8,128)(2,1)} %all-gather.7.cloned.1.call-done), kind=kOutput, calls=%fused_computation.16 | convolution fusion | flops 1610743808 | bytes 9699328 | tf_op jit(solution)/shard_map/dot_general | solution.py:56
  406.4 1.3 convolution_convert_fusion.3
  407.6 0.8 copy.27
  (11 shorter events, 0.1 us)
Async XLA Ops:
  6.5 1.1 copy-start
  9.4 35.9 %copy-start.2 = (bf16[192,256]{1,0:T(8,128)(2,1)S(1)}, bf16[192,256]{1,0:T(8,128)(2,1)}, u32[]{:S(2)}) copy-start(bf16[192,256]{1,0:T(8,128)(2,1)} %param.10) | copy-start | bytes 294916
  9.4 33.0 %all-to-all-start = ((bf16[32,32,384]{2,1,0:T(8,128)(2,1)}), bf16[32,32,384]{2,1,0:T(8,128)(2,1)S(1)}, u32[]{:S(2)}, u32[]{:S(2)}) async-start(bf16[32,32,384]{2,1,0:T(8,128)(2,1)} %broadcast_select_fusion), calls=%async_computation | async-start | bytes 1572864 | tf_op jit(solution)/shard_map/all_to_all | solution.py:29
  20.0 210.8 %all-gather.5.cloned.1.call-start = ((), (), s32[]{:S(2)}) async-start(), calls=%async_computation.2 | async-start | bytes 6684672 | tf_op jit(solution)/shard_map/all_gather | solution.py:41
  47.4 6.3 %copy-start.3 = (bf16[384]{0:T(512)(128)(2,1)S(1)}, bf16[384]{0:T(512)(128)(2,1)}, u32[]{:S(2)}) copy-start(bf16[384]{0:T(512)(128)(2,1)} %param.8) | copy-start | bytes 2308
  47.4 196.1 %all-to-all-start.1 = ((bf16[32,192,256]{2,1,0:T(8,128)(2,1)}), bf16[32,192,256]{2,1,0:T(8,128)(2,1)}, u32[]{:S(2)}, u32[]{:S(2)}) async-start(bf16[32,192,256]{2,1,0:T(8,128)(2,1)} %stack.2), calls=%async_computation.1 | async-start | bytes 6291456 | tf_op jit(solution)/shard_map/all_to_all | solution.py:13
  52.1 280.9 %all-gather.9.cloned.1.call-start = ((), (), s32[]{:S(2)}) async-start(), calls=%async_computation.4 | async-start | bytes 3244032 | tf_op jit(solution)/shard_map/all_gather | solution.py:51
  52.9 347.9 %all-gather.7.cloned.1.call-start = ((), (), s32[]{:S(2)}) async-start(), calls=%async_computation.3 | async-start | bytes 3244032 | tf_op jit(solution)/shard_map/all_gather | solution.py:53
  230.8 4.6 %copy-start.1 = (bf16[512,6144]{1,0:T(8,128)(2,1)S(1)}, bf16[512,6144]{1,0:T(8,128)(2,1)}, u32[]{:S(2)}) copy-start(bf16[512,6144]{1,0:T(8,128)(2,1)} %all-gather.5.cloned.1.call-done) | copy-start | bytes 18874372
Sparse Core Ops, SparseCore 0:
  45.5 185.3 all-gather.4
  233.0 100.0 all-gather.8
  335.2 65.5 all-gather.6
